TPU v7x, 512 devices: a whole 4x8x8 slice. The times are simulated.
512 devices in a mesh: row: 16 (over z, core), col: 32 (over y, x).
Axes of the slice: x: 4, y: 8, z: 8, core: 2. Of those that a mesh axis runs over, the one named last changes fastest.
Arguments:
- tokens: bfloat16 [4096, 2560], P('row', 'col'), may hold values from -6 to 6
- w_down: bfloat16 [2560, 1056], P('col'), may hold values from -0.125 to 0.125
- q_gain: float32 [768], replicated, may hold values from 0.1 to 1.9
- kv_gain: float32 [256], replicated, may hold values from 0.1 to 1.9
- w_q_up: bfloat16 [768, 3072], P(None, 'col'), may hold values from -8.8767604 to 8.8767604
- w_kv_up: bfloat16 [256, 4096], replicated, may hold values from -0.375 to 0.375
- w_out: bfloat16 [2048, 2560], P('col'), may hold values from -0.75 to 0.75
- latent_cache: bfloat16 [16, 8192, 288], P('row', 'col'), may hold values from -6 to 6
- cache_len: int32 [16], replicated, may hold values from 1 to 8192, as said below
- new_len: int32 [16], replicated, may hold values from 1 to 256, as said below
- page_table: int32 [16, 128], replicated, may hold values from 0 to 127, each once within a row
- home_slot: int32 [16], replicated, may hold values from 0 to 15, each once
Outputs:
- output: bfloat16 [4096, 2560], P('row', 'col')
Inputs may be any that keep to these rules, and one draw needn't show every extreme that they name: `cache_len`: some slot has exactly 8192 cached tokens; about half the slots hold at most 1024, the others at least 7168. `new_len`: some request has exactly 256 real new tokens.
All inputs are finite; a program needn't handle non-finite values.
Results may differ from a plain program's by a relative error of at most 0.023.
Values may be sent and summed in bfloat16 or wider, within the bound.
A program may use at most 64 MiB of HBM per device.

v0:
```python
import math
import jax
import jax.numpy as jnp
from jax import lax
from jax.sharding import PartitionSpec as P

NOPE = 64
ROPE = 32
VDIM = 64
epsilon = 1e-05


def rms_scale(values, gain):
    return values * lax.rsqrt(jnp.mean(values * values, axis=-1, keepdims=True) + epsilon) * gain


def angle_tables(positions, width):
    half_dim = width // 2
    frequency = 10000.0 ** (-2.0 * jnp.arange(half_dim, dtype=jnp.float32) / width)
    angles = positions.astype(jnp.float32)[:, None] * frequency[None, :]
    return (jnp.cos(angles), jnp.sin(angles))


def rotary(values, cosine, sine_table):
    half_dim = values.shape[-1] // 2
    first_half = values[..., :half_dim]
    second_half = values[..., half_dim:]
    return jnp.concatenate(
        [
            first_half * cosine - second_half * sine_table,
            second_half * cosine + first_half * sine_table,
        ],
        -1,
    )


def body(
    tokens,
    w_down,
    q_gain,
    kv_gain,
    w_q_up,
    w_kv_up,
    w_out,
    latent_cache,
    cache_len,
    new_len,
    page_table,
    home_slot,
):
    columns = lax.axis_size("col")
    column_id = lax.axis_index("col")
    row_id = lax.axis_index("row")
    group_rows = tokens.shape[0]
    own_rows = group_rows // columns
    q_width = q_gain.shape[0]
    kv_width = kv_gain.shape[0]
    slot_index = home_slot[row_id]
    cached_count = cache_len[slot_index]
    live_count = new_len[row_id]
    combined = lax.psum(jnp.dot(tokens, w_down, preferred_element_type=jnp.float32), "col")
    query_cos, query_sin = angle_tables(
        cached_count + jnp.arange(group_rows, dtype=jnp.int32), ROPE
    )
    query_latent = rms_scale(combined[:, :q_width], q_gain).astype(jnp.bfloat16)
    new_latent = rms_scale(combined[:, q_width : q_width + kv_width], kv_gain).astype(jnp.bfloat16)
    new_rope = rotary(combined[:, q_width + kv_width :], query_cos, query_sin).astype(jnp.bfloat16)
    fresh_latents = jnp.concatenate([new_latent, new_rope], 1)
    projected = jnp.dot(query_latent, w_q_up, preferred_element_type=jnp.float32)
    queries = jnp.concatenate(
        [projected[:, :NOPE], rotary(projected[:, NOPE:], query_cos, query_sin)], 1
    ).astype(jnp.bfloat16)
    segment = lax.all_gather(latent_cache, "row", axis=0, tiled=True)
    matches = jnp.arange(segment.shape[0], dtype=jnp.int32) == slot_index
    own_cache = jnp.sum(
        jnp.where(matches[:, None, None], segment.astype(jnp.float32), 0.0), 0
    ).astype(jnp.bfloat16)
    head_width = NOPE + VDIM
    head_weight = lax.dynamic_slice_in_dim(w_kv_up, column_id * head_width, head_width, 1)

    def expand(latents):
        lifted = jnp.dot(
            latents[:, :kv_width], head_weight, preferred_element_type=jnp.float32
        ).astype(jnp.bfloat16)
        return (jnp.concatenate([lifted[:, :NOPE], latents[:, kv_width:]], 1), lifted[:, NOPE:])

    cache_latents = lax.all_gather(own_cache, "col", axis=0, tiled=True)
    cache_keys, cache_values = expand(cache_latents)
    fresh_keys, fresh_values = expand(fresh_latents)
    key_total = cache_keys.shape[0]
    page_row = page_table[slot_index]
    page_count = page_row.shape[0]
    page_size = key_total // page_count
    block_size = min(512, key_total)
    offsets = jnp.arange(page_size, dtype=jnp.int32)
    page_ids = jnp.arange(page_count, dtype=jnp.int32)
    logical_page = jnp.sum(
        page_ids[:, None] * (page_row[:, None] == page_ids[None, :]).astype(jnp.int32), 0
    )
    cached_visible = (logical_page[:, None] * page_size + offsets[None, :]).reshape(
        key_total
    ) < cached_count
    block_limit = key_total // block_size
    score_scale = 1.0 / math.sqrt(NOPE + ROPE)
    query_index = jnp.arange(group_rows, dtype=jnp.int32)[:, None]
    key_index = jnp.arange(group_rows, dtype=jnp.int32)[None, :]
    fresh_visible = (key_index <= query_index) & (key_index < live_count)
    fresh_scores = (
        jnp.einsum("qd,kd->qk", queries, fresh_keys, preferred_element_type=jnp.float32)
        * score_scale
    )
    fresh_scores = jnp.where(fresh_visible, fresh_scores, -jnp.inf)
    first_peak = jnp.max(fresh_scores, 1)
    fresh_exponent = jnp.exp(fresh_scores - first_peak[:, None])
    start_state = (
        first_peak,
        jnp.sum(fresh_exponent, 1),
        jnp.dot(
            fresh_exponent.astype(jnp.bfloat16), fresh_values, preferred_element_type=jnp.float32
        ),
    )

    def accumulate(block_id, running):
        row_peak, row_total, summed = running
        key_block = lax.dynamic_slice_in_dim(cache_keys, block_id * block_size, block_size, 0)
        mask_block = lax.dynamic_slice_in_dim(cached_visible, block_id * block_size, block_size, 0)
        value_block = lax.dynamic_slice_in_dim(cache_values, block_id * block_size, block_size, 0)
        raw_scores = (
            jnp.einsum("qd,kd->qk", queries, key_block, preferred_element_type=jnp.float32)
            * score_scale
        )
        raw_scores = jnp.where(mask_block[None, :], raw_scores, -jnp.inf)
        next_peak = jnp.maximum(row_peak, jnp.max(raw_scores, 1))
        factor = jnp.exp(row_peak - next_peak)
        exponent = jnp.exp(raw_scores - next_peak[:, None])
        next_total = row_total * factor + jnp.sum(exponent, 1)
        next_summed = summed * factor[:, None] + jnp.dot(
            exponent.astype(jnp.bfloat16), value_block, preferred_element_type=jnp.float32
        )
        return (next_peak, next_total, next_summed)

    row_peak, row_total, summed = lax.fori_loop(0, block_limit, accumulate, start_state)
    attended = (summed / row_total[:, None]).astype(jnp.bfloat16)
    live_rows = jnp.arange(group_rows, dtype=jnp.int32) < live_count
    attended = jnp.where(live_rows[:, None], attended, jnp.zeros_like(attended))
    summed_out = lax.psum_scatter(
        lax.dot_general(
            w_out, attended, (((0,), (1,)), ((), ())), preferred_element_type=jnp.float32
        ).astype(jnp.bfloat16),
        "col",
        scatter_dimension=0,
        tiled=True,
    ).astype(jnp.float32)
    result = summed_out.T.astype(jnp.bfloat16)
    return result


def solution(mesh):
    return jax.shard_map(
        body,
        mesh=mesh,
        in_specs=(
            P("row", "col"),
            P("col", None),
            P(),
            P(),
            P(None, "col"),
            P(),
            P("col", None),
            P("row", "col", None),
            P(),
            P(),
            P(),
            P(),
        ),
        out_specs=P("row", "col"),
        check_vma=False,
    )
```

profile of v0, /device:TPU:16, one launch (start us, length us, event | category | flops | bytes accessed | tf_op | source)
XLA Modules:
  0.0 532.0 jit_solution(8802280258935113749)
XLA Ops:
  8.1 2.3 fusion.57
  11.8 46.3 %all-gather.3.cloned.1.call-done = bf16[16,256,288]{1,2,0:T(8,128)(2,1)} async-done(((bf16[1,256,288]{1,2,0:T(8,128)(2,1)}), bf16[16,256,288]{1,2,0:T(8,128)(2,1)}) %all-gather.3.cloned.1.call-update) | async-done | bytes 2359312 | tf_op jit(solution)/shard_map/all_gather | solution.py:73
  58.2 2.9 select_reduce_fusion
  67.2 109.0 %all-reduce.2.cloned.1.call-done = f32[256,1056]{0,1:T(8,128)} async-done(((f32[256,1056]{0,1:T(8,128)}), f32[256,1056]{0,1:T(8,128)}) %all-reduce.2.cloned.1.call-update) | async-done | bytes 1081360 | tf_op jit(solution)/shard_map/psum | solution.py:61
  176.2 1.0 multiply_reduce_fusion.1
  177.3 1.2 convolution_convert_fusion.2
  178.5 1.3 multiply_reduce_fusion
  179.8 1.4 fusion.12
  181.2 0.9 fusion.42
  182.7 84.2 %all-gather.5.cloned.1.call-done = bf16[8192,288]{0,1:T(8,128)(2,1)} async-done(((bf16[256,288]{0,1:T(8,128)(2,1)}), bf16[8192,288]{0,1:T(8,128)(2,1)}) %all-gather.5.cloned.1.call-update) | async-done | bytes 4718608 | tf_op jit(solution)/shard_map/all_gather | solution.py:87
  266.9 2.9 convolution_convert_fusion
  270.9 1.3 pad_maximum_fusion
  272.2 26.9 %while.17 = (s32[]{:T(128)}, f32[256]{0:T(256)S(1)}, f32[256]{0:T(256)S(1)}, f32[256,64]{0,1:T(8,128)S(1)}, pred[8192]{0:T(1024)(128)(4,1)S(1)}, /*index=5*/bf16...) while((s32[]{:T(128)}, f32[256]{0:T(256)S(1)}, ...), condition=%wide.region_10.11_spmd, body=%wide.region_7.10_spmd.sunk | while | flops 42893828 | bytes 1935023 | solution.py:142
  272.3 1.2 fusion.71
  273.9 1.2 fusion.71
  275.6 1.2 fusion.71
  277.3 1.2 fusion.71
  279.0 1.2 fusion.71
  280.7 1.2 fusion.71
  282.4 1.2 fusion.71
  284.1 1.2 fusion.71
  285.7 1.2 fusion.71
  287.4 1.2 fusion.71
  289.1 1.2 fusion.71
  290.8 1.2 fusion.71
  292.5 1.2 fusion.71
  294.2 1.2 fusion.71
  295.8 1.2 fusion.71
  297.5 1.2 fusion.71
  299.1 1.5 fusion.10
  300.6 1.5 copy.29
  302.1 222.3 %reduce-scatter.4.cloned.1.call-done = bf16[80,256]{1,0:T(8,128)(2,1)} async-done(((bf16[2560,256]{1,0:T(8,128)(2,1)}), bf16[80,256]{1,0:T(8,128)(2,1)}) %reduce-scatter.4.cloned.1.call-update) | async-done | bytes 40976
  (142 shorter events, 15.4 us)
Async XLA Ops:
  7.4 169.9 %copy-start = (bf16[256,4096]{1,0:T(8,128)(2,1)S(1)}, bf16[256,4096]{1,0:T(8,128)(2,1)}, u32[]{:S(2)}) copy-start(bf16[256,4096]{1,0:T(8,128)(2,1)} %param.19) | copy-start | bytes 6291460
  7.4 3.2 copy-start.4
  7.4 50.8 %all-gather.3.cloned.1.call-start = ((), (), s32[]{:S(2)}) async-start(), calls=%async_computation.2 | async-start | bytes 2506752 | tf_op jit(solution)/shard_map/all_gather | solution.py:73
  8.1 168.1 %all-reduce.2.cloned.1.call-start = ((), (), s32[]{:S(2)}) async-start(), calls=%async_computation.1 | async-start | bytes 2162688 | tf_op jit(solution)/shard_map/psum | solution.py:61
  10.5 52.0 %copy-start.5 = (s32[16]{0:T(128)S(1)}, s32[16]{0:T(128)}, u32[]{:S(2)}) copy-start(s32[16]{0:T(128)} %param.23) | copy-start | bytes 196
  10.5 53.3 %copy-start.6 = (s32[16]{0:T(128)S(1)}, s32[16]{0:T(128)}, u32[]{:S(2)}) copy-start(s32[16]{0:T(128)} %param.22) | copy-start | bytes 196
  10.5 166.8 %copy-start.3 = (f32[256]{0:T(256)S(1)}, f32[256]{0:T(256)}, u32[]{:S(2)}) copy-start(f32[256]{0:T(256)} %param.17) | copy-start | bytes 3076
  10.5 256.4 %all-gather.5.cloned.1.call-start = ((), (), s32[]{:S(2)}) async-start(), calls=%async_computation.3 | async-start | bytes 4866048 | tf_op jit(solution)/shard_map/all_gather | solution.py:87
  11.8 167.9 %copy-start.1 = (bf16[768,96]{0,1:T(8,128)(2,1)S(1)}, bf16[768,96]{0,1:T(8,128)(2,1)}, u32[]{:S(2)}) copy-start(bf16[768,96]{0,1:T(8,128)(2,1)} %param.18) | copy-start | bytes 442372
  11.8 167.9 %copy-start.2 = (f32[768]{0:T(1024)S(1)}, f32[768]{0:T(1024)}, u32[]{:S(2)}) copy-start(f32[768]{0:T(1024)} %param.16) | copy-start | bytes 9220
  61.1 463.3 %reduce-scatter.4.cloned.1.call-start = ((), (), s32[]{:S(2)}) async-start(), calls=%async_computation.4 | async-start | bytes 1351680
  269.9 1.0 slice-start
Sparse Core Ops, SparseCore 0:
  10.3 47.8 all-gather.2
Sparse Core Ops, SparseCore 1:
  12.0 164.2 all-reduce.1
  179.2 87.7 all-gather.4
  302.2 222.2 reduce-scatter.3
where the time goes:
time: 533 us; the launch traced here: 532 us
  waiting for transfers between devices  463 us (87%)
  matrix products  32.4 us (6%)
  between operations  17.1 us (3%)
  other arithmetic  12.4 us (2%)
  local copies, waits for them, and re-layouts  6.62 us (1%)
    unnamed x5, waiting for transfers between devices  223 us
    psum x1, waiting for transfers between devices, body(): lax.psum(jnp.dot(tokens, w_down, preferred_element_type=jnp.float32), 'col')  109 us
    all_gather x1, waiting for transfers between devices, body(): cache_latents = lax.all_gather(own_cache, 'col', axis=0, tiled=True)  84.2 us
    all_gather x1, waiting for transfers between devices, body(): segment = lax.all_gather(latent_cache, 'row', axis=0, tiled=True)  46.3 us
    dot_general x16, matrix products, accumulate(): jnp.einsum('qd,kd->qk', queries, key_block, preferred_element_type=jnp.fl...  18.8 us
  transfers between devices with their start and end apart: 4, of which 4 were waited for; matrix products, arithmetic and copies ran while one was open for 3% of the time, Pallas kernels for 0%

commit v1 on v0

--- a/solution.py
+++ b/solution.py
@@ -58,7 +58,14 @@
     slot_index = home_slot[row_id]
     cached_count = cache_len[slot_index]
     live_count = new_len[row_id]
-    combined = lax.psum(jnp.dot(tokens, w_down, preferred_element_type=jnp.float32), "col")
+
+    def run_types(q_in, axis_name):
+        d_next = lax.all_gather(q_in, axis_name).sum(axis=0)
+        return d_next
+
+    combined = run_types(
+        jnp.dot(tokens, w_down, preferred_element_type=jnp.float32), axis_name="col"
+    )
     query_cos, query_sin = angle_tables(
         cached_count + jnp.arange(group_rows, dtype=jnp.int32), ROPE
     )

time: 533 us -> 691 us (1.30)
  waiting for transfers between devices: 463 us -> 602 us
  local copies, waits for them, and re-layouts: 6.62 us -> 27.7 us
    all_gather x0 -> x1, waiting for transfers between devices: none -> 254 us  [run_types(): d_next = lax.all_gather(q_in, axis_name).sum(axis=0)]
    psum x1 -> x0, waiting for transfers between devices: 109 us -> none  [body(): lax.psum(jnp.dot(tokens, w_down, preferred_element_type=jnp.float32), 'col')]
    unnamed x15 -> x18, local copies, waits for them, and re-layouts: 1.49 us -> 22 us
  transfers between devices with their start and end apart: 4 -> 4, of which waited for: 4 -> 4; matrix products, arithmetic and copies ran while one was open for 3% -> 2% of each run, Pallas kernels for 0% -> 0%
where the time goes in v1:
time: 691 us; the launch traced here: 690 us
  waiting for transfers between devices  602 us (87%)
  matrix products  29.3 us (4%)
  local copies, waits for them, and re-layouts  27.7 us (4%)
  other arithmetic  15.1 us (2%)
  between operations  15.1 us (2%)
    all_gather x1, waiting for transfers between devices, run_types(): d_next = lax.all_gather(q_in, axis_name).sum(axis=0)  254 us
    unnamed x5, waiting for transfers between devices  219 us
    all_gather x1, waiting for transfers between devices, body(): cache_latents = lax.all_gather(own_cache, 'col', axis=0, tiled=True)  80.3 us
    all_gather x1, waiting for transfers between devices, body(): segment = lax.all_gather(latent_cache, 'row', axis=0, tiled=True)  48.2 us
    unnamed x18, local copies, waits for them, and re-layouts  22 us
    dot_general x16, matrix products, accumulate(): jnp.einsum('qd,kd->qk', queries, key_block, preferred_element_type=jnp.fl...  18.7 us
  transfers between devices with their start and end apart: 4, of which 4 were waited for; matrix products, arithmetic and copies ran while one was open for 2% of the time, Pallas kernels for 0%

profile of v1, /device:TPU:16, one launch (start us, length us, event | category | flops | bytes accessed | tf_op | source)
XLA Modules:
  0.0 690.0 jit_solution(6567342313598170820)
XLA Ops:
  6.5 0.7 all-gather.5.cloned.1.call-update
  7.3 1.2 dynamic_slice.37
  9.2 48.2 %all-gather.5.cloned.1.call-done = bf16[16,256,288]{1,2,0:T(8,128)(2,1)} async-done(((bf16[1,256,288]{1,2,0:T(8,128)(2,1)}), bf16[16,256,288]{1,2,0:T(8,128)(2,1)}) %all-gather.5.cloned.1.call-update) | async-done | bytes 2359312 | tf_op jit(solution)/shard_map/all_gather | solution.py:80
  57.4 2.9 select_reduce_fusion
  60.4 1.3 fusion.57
  67.5 80.3 %all-gather.7.cloned.1.call-done = bf16[8192,288]{0,1:T(8,128)(2,1)} async-done(((bf16[256,288]{0,1:T(8,128)(2,1)}), bf16[8192,288]{0,1:T(8,128)(2,1)}) %all-gather.7.cloned.1.call-update) | async-done | bytes 4718608 | tf_op jit(solution)/shard_map/all_gather | solution.py:94
  147.8 2.9 convolution_convert_fusion
  150.9 0.9 slice-done
  151.8 1.2 pad_maximum_fusion
  153.1 254.5 %all-gather.9.cloned.1.call-done = f32[8192,1056]{0,1:T(8,128)} async-done(((f32[256,1056]{0,1:T(8,128)}), f32[8192,1056]{0,1:T(8,128)}) %all-gather.9.cloned.1.call-update) | async-done | bytes 34603024 | tf_op jit(solution)/shard_map/all_gather | solution.py:63
  407.5 20.5 %copy.34 = f32[132,8,32,256]{3,2,1,0:T(8,128)S(1)} copy(f32[132,8,32,256]{3,1,2,0:T(8,128)} %bitcast.22) | data formatting | bytes 69206016
  428.0 5.7 bitcast_reduce_fusion
  435.3 26.7 %while.17 = (s32[]{:T(128)}, f32[256]{0:T(256)S(1)}, f32[256]{0:T(256)S(1)}, f32[256,64]{0,1:T(8,128)S(1)}, pred[8192]{0:T(1024)(128)(4,1)S(1)}, /*index=5*/bf16...) while((s32[]{:T(128)}, f32[256]{0:T(256)S(1)}, ...), condition=%wide.region_10.11_spmd, body=%wide.region_7.10_spmd.sunk | while | flops 42893828 | bytes 1935031 | solution.py:149
  435.4 1.2 fusion.71
  437.1 1.2 fusion.71
  438.8 1.2 fusion.71
  440.5 1.2 fusion.71
  442.1 1.2 fusion.71
  443.8 1.2 fusion.71
  445.5 1.2 fusion.71
  447.1 1.2 fusion.71
  448.8 1.2 fusion.71
  450.5 1.2 fusion.71
  452.2 1.2 fusion.71
  453.8 1.2 fusion.71
  455.5 1.2 fusion.71
  457.2 1.2 fusion.71
  458.8 1.2 fusion.71
  460.5 1.2 fusion.71
  462.1 1.5 fusion.10
  463.6 1.5 copy.29
  465.1 218.4 %reduce-scatter.4.cloned.1.call-done = bf16[80,256]{1,0:T(8,128)(2,1)} async-done(((bf16[2560,256]{1,0:T(8,128)(2,1)}), bf16[80,256]{1,0:T(8,128)(2,1)}) %reduce-scatter.4.cloned.1.call-update) | async-done | bytes 40976
  (146 shorter events, 13.8 us)
Async XLA Ops:
  6.5 141.3 %copy-start = (bf16[256,4096]{1,0:T(8,128)(2,1)S(1)}, bf16[256,4096]{1,0:T(8,128)(2,1)}, u32[]{:S(2)}) copy-start(bf16[256,4096]{1,0:T(8,128)(2,1)} %param.19) | copy-start | bytes 6291460
  6.5 53.8 %copy-start.3 = (bf16[256,80]{0,1:T(8,128)(2,1)S(1)}, bf16[256,80]{0,1:T(8,128)(2,1)}, u32[]{:S(2)}) copy-start(bf16[256,80]{0,1:T(8,128)(2,1)} %param.14) | copy-start | bytes 122884
  6.5 53.8 %copy-start.1 = (bf16[80,1056]{1,0:T(8,128)(2,1)S(1)}, bf16[80,1056]{1,0:T(8,128)(2,1)}, u32[]{:S(2)}) copy-start(bf16[80,1056]{1,0:T(8,128)(2,1)} %param.15) | copy-start | bytes 506884
  6.5 50.8 %all-gather.5.cloned.1.call-start = ((), (), s32[]{:S(2)}) async-start(), calls=%async_computation.1 | async-start | bytes 2506752 | tf_op jit(solution)/shard_map/all_gather | solution.py:80
  7.3 140.6 %all-gather.7.cloned.1.call-start = ((), (), s32[]{:S(2)}) async-start(), calls=%async_computation.2 | async-start | bytes 4866048 | tf_op jit(solution)/shard_map/all_gather | solution.py:94
  9.1 53.8 %copy-start.6 = (s32[16]{0:T(128)S(1)}, s32[16]{0:T(128)}, u32[]{:S(2)}) copy-start(s32[16]{0:T(128)} %param.23) | copy-start | bytes 196
  9.2 55.0 %copy-start.7 = (s32[16]{0:T(128)S(1)}, s32[16]{0:T(128)}, u32[]{:S(2)}) copy-start(s32[16]{0:T(128)} %param.22) | copy-start | bytes 196
  60.3 347.3 %all-gather.9.cloned.1.call-start = ((), (), s32[]{:S(2)}) async-start(), calls=%async_computation.3 | async-start | bytes 35684352 | tf_op jit(solution)/shard_map/all_gather | solution.py:63
  61.7 621.8 %reduce-scatter.4.cloned.1.call-start = ((), (), s32[]{:S(2)}) async-start(), calls=%async_computation.4 | async-start | bytes 1351680
  150.8 1.0 slice-start
  428.0 5.9 copy-start.5
  428.0 6.2 copy-start.2
  428.0 6.2 copy-start.4
Sparse Core Ops, SparseCore 0:
  9.5 47.8 all-gather.4
  60.4 87.3 all-gather.6
  150.9 256.6 all-gather.8
  465.2 218.2 reduce-scatter.3
